TPU v7x, 128 devices: a whole 4x4x4 slice. The times are simulated.
128 devices in a mesh: frames: 4 (over z_lo, core), rows: 32 (over z_hi, y, x).
Axes of the slice: x: 4, y: 4, z: 4 (z_hi: 2, z_lo: 2; z = z_hi * 2 + z_lo), core: 2. Of those that a mesh axis runs over, the one named last changes fastest.
Arguments:
- clip_in: bfloat16 [16, 128, 64, 256], P('frames', 'rows'), may hold values from -6 to 6
- kernel_one: bfloat16 [3, 3, 3, 64, 64], replicated, may hold values from -0.15625 to 0.15625
- bias_one: float32 [64], replicated, may hold values from -3 to 3
- kernel_two: bfloat16 [3, 3, 3, 64, 64], replicated, may hold values from -0.3125 to 0.3125
- cotangent: bfloat16 [16, 128, 64, 256], P('frames', 'rows'), may hold values from -6 to 6
Outputs:
- block_out: bfloat16 [16, 128, 64, 256], P('frames', 'rows')
- grad_input: bfloat16 [16, 128, 64, 256], P('frames', 'rows')
- grad_first: float32 [3, 3, 3, 64, 64], replicated
- grad_second: float32 [3, 3, 3, 64, 64], replicated
- grad_bias: float32 [64], replicated
All inputs are finite; a program needn't handle non-finite values.
Results may differ from a plain program's by a relative error of at most 0.0065.
Values may be sent and summed in bfloat16 or wider, within the bound.
No kernel may reach another device: no remote copies, remote signals or barrier semaphores. Data moves between devices by JAX's collectives and lax.ppermute only.
A program may use at most 64 MiB of HBM per device.

v0:
```python
import math
import jax
import jax.numpy as jnp
from jax import lax
from jax.sharding import PartitionSpec as P


def with_halo(block, sides, width):
    for axis, dim in sides:
        count = lax.axis_size(axis)
        forward = [(i, i + 1) for i in range(count - 1)]
        backward = [(target, source) for source, target in forward]
        low = lax.ppermute(
            lax.slice_in_dim(block, block.shape[dim] - width, None, axis=dim), axis, forward
        )
        high = lax.ppermute(lax.slice_in_dim(block, 0, width, axis=dim), axis, backward)
        block = jnp.concatenate([low, block, high], axis=dim)
    return block


def passed_along(value, axis, by):
    devices = lax.axis_size(axis)
    pairs = [(i, i + by) for i in range(devices) if 0 <= i + by < devices]
    return lax.ppermute(value, axis, pairs)


def extend_rows(field):
    return with_halo(field, (("rows", 1),), 1)


def with_prior(field):
    earlier = passed_along(field[-2:], "frames", 1)
    return jnp.concatenate([earlier, field], axis=0)


def with_later(field):
    following = passed_along(field[:2], "frames", -1)
    return jnp.concatenate([field, following], axis=0)


def spatial_taps(extended, row_count, col_count, flipped):
    padded = jnp.pad(extended, ((0, 0), (0, 0), (0, 0), (1, 1)))
    pieces = []
    for i in range(3):
        for j in range(3):
            row_start = 2 - i if flipped else i
            col_start = 2 - j if flipped else j
            pieces.append(
                padded[:, row_start : row_start + row_count, :, col_start : col_start + col_count]
            )
    return jnp.concatenate(pieces, axis=2)


def forward_conv(extended, kernel, frame_count, row_count, col_count):
    taps = spatial_taps(extended, row_count, col_count, False)
    chan_out = kernel.shape[3]
    running = None
    for t in range(3):
        flat_kernel = jnp.transpose(kernel[t], (2, 0, 1, 3)).reshape((chan_out, -1))
        term = jnp.einsum(
            "ok,frkw->frow",
            flat_kernel,
            taps[t : t + frame_count],
            preferred_element_type=jnp.float32,
        )
        running = term if running is None else running + term
    return running


def adjoint_conv(extended, kernel, frame_count, row_count, col_count):
    taps = spatial_taps(extended, row_count, col_count, True)
    chan_in = kernel.shape[4]
    running = None
    for t in range(3):
        flat_kernel = jnp.transpose(kernel[t], (3, 0, 1, 2)).reshape((chan_in, -1))
        term = jnp.einsum(
            "ck,frkw->frcw",
            flat_kernel,
            taps[2 - t : 2 - t + frame_count],
            preferred_element_type=jnp.float32,
        )
        running = term if running is None else running + term
    return running


def kernel_grad(upstream, extended):
    frame_count, row_count, chan_out, col_count = upstream.shape
    chan_in = extended.shape[2]
    taps = spatial_taps(extended, row_count, col_count, False)
    pieces = []
    for t in range(3):
        flat = jnp.einsum(
            "frow,frkw->ok", upstream, taps[t : t + frame_count], preferred_element_type=jnp.float32
        )
        pieces.append(jnp.transpose(flat.reshape((chan_out, 3, 3, chan_in)), (1, 2, 0, 3)))
    return jnp.stack(pieces, axis=0)


def per_device(clip_in, kernel_one, bias_one, kernel_two, cotangent):
    frame_count, row_count, channels, col_count = clip_in.shape
    input_rows = extend_rows(clip_in)
    cot_rows = None
    input_ext = with_prior(input_rows)
    hidden = (
        forward_conv(input_ext, kernel_one, frame_count, row_count, col_count)
        + bias_one[None, None, :, None]
    )
    active = jax.nn.silu(hidden).astype(jnp.bfloat16)
    active_ext = with_prior(extend_rows(active))
    block_out = (
        clip_in.astype(jnp.float32)
        + forward_conv(active_ext, kernel_two, frame_count, row_count, col_count)
    ).astype(jnp.bfloat16)
    cot_rows = extend_rows(cotangent)
    cot_ext = with_later(cot_rows)
    grad_act = adjoint_conv(cot_ext, kernel_two, frame_count, row_count, col_count)
    sig = jax.nn.sigmoid(hidden)
    grad_pre = (grad_act * sig * (1.0 + hidden * (1.0 - sig))).astype(jnp.bfloat16)
    pre_ext = with_later(extend_rows(grad_pre))
    grad_back = adjoint_conv(pre_ext, kernel_one, frame_count, row_count, col_count)
    grad_input = (cotangent.astype(jnp.float32) + grad_back).astype(jnp.bfloat16)
    term_second = kernel_grad(cotangent, active_ext)
    term_first = kernel_grad(grad_pre, input_ext)
    term_bias = jnp.sum(grad_pre.astype(jnp.float32), axis=(0, 1, 3))
    total_first, total_second, total_bias = lax.psum(
        (term_first, term_second, term_bias), ("frames", "rows")
    )
    cell_total = (
        frame_count * lax.axis_size("frames") * row_count * lax.axis_size("rows") * col_count
    )
    inv_scale = 1.0 / math.sqrt(cell_total)
    return (
        block_out,
        grad_input,
        total_first * inv_scale,
        total_second * inv_scale,
        total_bias * inv_scale,
    )


def solution(mesh):
    in_specs = (P("frames", "rows", None, None), P(), P(), P(), P("frames", "rows", None, None))
    out_specs = (P("frames", "rows", None, None), P("frames", "rows", None, None), P(), P(), P())
    return jax.shard_map(
        per_device, mesh=mesh, in_specs=in_specs, out_specs=out_specs, check_vma=False
    )
```

profile of v0, /device:TPU:1, one launch (start us, length us, event | category | flops | bytes accessed | tf_op | source)
XLA Modules:
  0.0 345.2 jit_solution(11832718589891835297)
XLA Ops:
  7.2 1.7 fusion.59
  9.0 1.3 collective-permute-start.1
  10.2 5.2 %collective-permute-start = (bf16[4,1,64,256]{3,2,1,0:T(8,128)(2,1)}, bf16[4,1,64,256]{3,2,1,0:T(8,128)(2,1)}, u32[]{:S(2)}, u32[]{:S(2)}) collective-permute-start(bf16[4,1,64,256]{3,2,1,0:T(8,128)(2,1)} %get-tuple-element.19), channel_id=1, source_target_pairs={{0,1},{1,2},{2,3},{3,4},{4,5},{5,6},{6,7},{7,8},{8,9},{9,10},{10,1... | collective-permute-start | bytes 393224 | tf_op jit(solution)/shard_map/ppermute | solution.py:13
  15.5 1.0 fusion.57
  16.5 1.3 collective-permute-start.7
  17.8 4.0 %collective-permute-start.6 = (bf16[4,1,64,256]{3,2,1,0:T(8,128)(2,1)S(1)}, bf16[4,1,64,256]{3,2,1,0:T(8,128)(2,1)S(1)}, u32[]{:S(2)}, u32[]{:S(2)}) collective-permute-start(bf16[4,1,64,256]{3,2,1,0:T(8,128)(2,1)S(1)} %get-tuple-element.15), channel_id=1, source_target_pairs={{0,1},{1,2},{2,3},{3,4},{4,5},{5,6},{6,7},{7,8},{8,9},{9,10},{10,1... | collective-permute-start | bytes 393224 | tf_op jit(solution)/shard_map/ppermute | solution.py:13
  21.8 2.0 fusion.60
  23.7 1.1 constant_dynamic-update-slice_fusion.4
  24.9 4.4 %collective-permute-start.8 = (bf16[2,6,64,256]{3,2,1,0:T(8,128)(2,1)S(1)}, bf16[2,6,64,256]{3,2,1,0:T(8,128)(2,1)S(1)}, u32[]{:S(2)}, u32[]{:S(2)}) collective-permute-start(bf16[2,6,64,256]{3,2,1,0:T(8,128)(2,1)S(1)} %slice.318), channel_id=1, source_target_pairs={{32,0},{64,32},{96,64},{33,1},{65,33},{97,65},{34,2},{66,34},{98,6... | collective-permute-start | bytes 1179656 | tf_op jit(solution)/shard_map/ppermute | solution.py:24
  29.3 1.9 fusion.61
  31.2 0.8 copy.28
  32.6 0.8 copy.38
  33.4 0.9 constant_dynamic-update-slice_fusion.2
  34.4 3.6 %collective-permute-start.2 = (bf16[2,6,64,256]{3,2,1,0:T(8,128)(2,1)S(1)}, bf16[2,6,64,256]{3,2,1,0:T(8,128)(2,1)S(1)}, u32[]{:S(2)}, u32[]{:S(2)}) collective-permute-start(bf16[2,6,64,256]{3,2,1,0:T(8,128)(2,1)S(1)} %slice.306), channel_id=1, source_target_pairs={{0,32},{32,64},{64,96},{1,33},{33,65},{65,97},{2,34},{34,66},{66,9... | collective-permute-start | bytes 1179656 | tf_op jit(solution)/shard_map/ppermute | solution.py:24
  38.8 0.3 fusion.46
  39.5 0.3 fusion.48
  40.3 1.0 fusion.66
  41.3 1.0 fusion.65
  42.4 2.6 collective-permute-done.2
  45.5 0.3 fusion.33
  46.2 0.3 fusion.35
  47.0 0.3 fusion.37
  47.3 1.1 fusion.63
  48.4 1.0 fusion.62
  49.5 1.3 multiply_convert_fusion
  50.7 1.5 convert_reduce_fusion
  52.2 1.4 fusion
  53.6 2.1 fusion.2
  55.7 2.1 fusion.4
  57.8 1.8 collective-permute-start.3
  59.6 1.3 collective-permute-start.4
  61.0 4.0 %collective-permute-start.9 = (bf16[4,1,64,256]{3,2,1,0:T(8,128)(2,1)S(1)}, bf16[4,1,64,256]{3,2,1,0:T(8,128)(2,1)S(1)}, u32[]{:S(2)}, u32[]{:S(2)}) collective-permute-start(bf16[4,1,64,256]{3,2,1,0:T(8,128)(2,1)S(1)} %get-tuple-element.12), channel_id=1, source_target_pairs={{0,1},{1,2},{2,3},{3,4},{4,5},{5,6},{6,7},{7,8},{8,9},{9,10},{10,1... | collective-permute-start | bytes 393224 | tf_op jit(solution)/shard_map/ppermute | solution.py:13
  65.0 1.3 collective-permute-start.10
  66.3 92.7 %psum.23 = f32[64]{0:T(128)S(1)} all-reduce(f32[64]{0:T(128)S(1)} %get-tuple-element.34), channel_id=1, replica_groups=mesh['frames'=4,'rows'=32] {'frames','rows'}, use_global_device_ids=true, to_apply=%region_3.4 | all-reduce | flops 64 | bytes 512 | tf_op jit(solution)/shard_map/psum | solution.py:125
  159.0 3.9 %collective-permute-start.5 = (bf16[2,6,64,256]{3,2,1,0:T(8,128)(2,1)S(1)}, bf16[2,6,64,256]{3,2,1,0:T(8,128)(2,1)S(1)}, u32[]{:S(2)}, u32[]{:S(2)}) collective-permute-start(bf16[2,6,64,256]{3,2,1,0:T(8,128)(2,1)S(1)} %pad_maximum_fusion.7), channel_id=1, source_target_pairs={{0,32},{32,64},{64,96},{1,33},{33,65},{65,97},{2,34},{34,66},{66,9... | collective-permute-start | bytes 1179656 | tf_op jit(solution)/shard_map/ppermute | solution.py:24
  163.0 0.5 broadcast_multiply_fusion.2
  163.5 2.1 pad_maximum_fusion.3
  165.6 0.8 pad_maximum_fusion.5
  166.4 2.1 collective-permute-start.11
  169.0 0.3 fusion.39
  169.4 0.3 fusion.40
  169.8 0.3 fusion.41
  170.1 0.3 fusion.42
  170.5 0.3 fusion.43
  170.9 1.5 convolution_bitcast_fusion
  172.4 1.5 convolution_bitcast_fusion.1
  173.9 1.5 convolution_bitcast_fusion.2
  175.9 4.4 %fusion.64 = f32[4,4,256,64]{2,3,1,0:T(8,128)} fusion(bf16[6,4,576,256]{3,2,1,0:T(8,128)(2,1)} %copy-done, bf16[64,576,1,1]{0,1,3,2:T(8,128)(2,1)S(1)} %bitcast.194), kind=kOutput, calls=%fused_computation.143 | convolution fusion | flops 301989888 | bytes 8200192 | tf_op jit(solution)/shard_map/ok,frkw->frow/dot_general | solution.py:60
  180.8 0.3 fusion.51
  181.1 0.3 fusion.52
  181.5 0.3 fusion.53
  181.8 0.3 fusion.54
  182.3 0.3 fusion.55
  182.6 2.9 copy-done.1
  185.5 1.0 pad_maximum_fusion.4
  186.6 3.9 %convolution_add_fusion.4 = f32[4,4,256,64]{2,3,1,0:T(8,128)S(1)} fusion(f32[4,4,256,64]{2,3,1,0:T(8,128)} %fusion.64, bf16[6,4,576,256]{3,2,1,0:T(8,128)(2,1)} %copy-done, bf16[64,576,1,1]{0,1,3,2:T(8,128)(2,1)S(1)} %bitcast.192), kind=kOutput, calls=%fused_computation.44 | convolution fusion | flops 302252032 | bytes 9248768 | tf_op jit(solution)/shard_map/ok,frkw->frow/dot_general | solution.py:60
  190.4 4.5 %fusion.19 = bf16[4,4,64,256]{3,2,1,0:T(8,128)(2,1)} fusion(f32[4,4,256,64]{2,3,1,0:T(8,128)S(1)} %convolution_add_fusion.4, bf16[6,4,576,256]{3,2,1,0:T(8,128)(2,1)} %copy-done, bf16[64,576,1,1]{0,1,3,2:T(8,128)(2,1)} %bitcast.193, bf16[4,4,64,256]{3,2,1,0:T(8,128)(2,1)S(1)} %copy-done.4), kind=kOutput, calls=%fused_computation.63 | convolution fusion | flops 303038464 | bytes 9248768 | tf_op jit(solution)/shard_map/ok,frkw->frow/dot_general | solution.py:60
  195.0 1.1 fusion.67
  196.0 1.1 convolution_add_fusion.1
  197.1 1.9 fusion.17
  199.0 135.3 %all-reduce.7.cloned.1.call-done = (f32[3,3,3,64,64]{3,4,2,1,0:T(8,128)}, f32[3,3,3,64,64]{3,4,2,1,0:T(8,128)}) async-done(((f32[3,3,3,64,64]{3,4,2,1,0:T(8,128)}, f32[3,3,3,64,64]{3,4,2,1,0:T(8,128)}), (f32[3,3,3,64,64]{3,4,2,1,0:T(8,128)}, f32[3,3,3,64,64]{3,4,2,1,0:T(8,128)})) %all-reduce.7.cloned.1.call-update) | async-done | bytes 884752 | tf_op jit(solution)/shard_map/psum | solution.py:125
  334.3 1.6 broadcast_multiply_fusion
  335.9 1.2 copy.53
  337.1 1.2 copy.52
  (80 shorter events, 5.5 us)
Async XLA Ops:
  7.2 27.2 %copy-start.3 = (bf16[4,4,64,256]{3,2,1,0:T(8,128)(2,1)S(1)}, bf16[4,4,64,256]{3,2,1,0:T(8,128)(2,1)}, u32[]{:S(2)}) copy-start(bf16[4,4,64,256]{3,2,1,0:T(8,128)(2,1)} %param.5) | copy-start | bytes 1572868
  7.2 327.1 %all-reduce.7.cloned.1.call-start = ((), (), s32[]{:S(2)}) async-start(), calls=%async_computation | async-start | bytes 3538944 | tf_op jit(solution)/shard_map/psum | solution.py:125
  9.0 25.4 %collective-permute-start.1 = (bf16[4,1,64,256]{3,2,1,0:T(8,128)(2,1)}, bf16[4,1,64,256]{3,2,1,0:T(8,128)(2,1)S(1)}, u32[]{:S(2)}, u32[]{:S(2)}) collective-permute-start(bf16[4,1,64,256]{3,2,1,0:T(8,128)(2,1)} %get-tuple-element.18), channel_id=1, source_target_pairs={{1,0},{2,1},{3,2},{4,3},{5,4},{6,5},{7,6},{8,7},{9,8},{10,9},{11,1... | collective-permute-start | bytes 393224 | tf_op jit(solution)/shard_map/ppermute | solution.py:16
  10.2 23.2 %collective-permute-start = (bf16[4,1,64,256]{3,2,1,0:T(8,128)(2,1)}, bf16[4,1,64,256]{3,2,1,0:T(8,128)(2,1)}, u32[]{:S(2)}, u32[]{:S(2)}) collective-permute-start(bf16[4,1,64,256]{3,2,1,0:T(8,128)(2,1)} %get-tuple-element.19), channel_id=1, source_target_pairs={{0,1},{1,2},{2,3},{3,4},{4,5},{5,6},{6,7},{7,8},{8,9},{9,10},{10,1... | collective-permute-start | bytes 393224 | tf_op jit(solution)/shard_map/ppermute | solution.py:13
  16.5 8.4 %collective-permute-start.7 = (bf16[4,1,64,256]{3,2,1,0:T(8,128)(2,1)S(1)}, bf16[4,1,64,256]{3,2,1,0:T(8,128)(2,1)S(1)}, u32[]{:S(2)}, u32[]{:S(2)}) collective-permute-start(bf16[4,1,64,256]{3,2,1,0:T(8,128)(2,1)S(1)} %get-tuple-element.14), channel_id=1, source_target_pairs={{1,0},{2,1},{3,2},{4,3},{5,4},{6,5},{7,6},{8,7},{9,8},{10,9},{11,1... | collective-permute-start | bytes 393224 | tf_op jit(solution)/shard_map/ppermute | solution.py:16
  17.8 6.0 %collective-permute-start.6 = (bf16[4,1,64,256]{3,2,1,0:T(8,128)(2,1)S(1)}, bf16[4,1,64,256]{3,2,1,0:T(8,128)(2,1)S(1)}, u32[]{:S(2)}, u32[]{:S(2)}) collective-permute-start(bf16[4,1,64,256]{3,2,1,0:T(8,128)(2,1)S(1)} %get-tuple-element.15), channel_id=1, source_target_pairs={{0,1},{1,2},{2,3},{3,4},{4,5},{5,6},{6,7},{7,8},{8,9},{9,10},{10,1... | collective-permute-start | bytes 393224 | tf_op jit(solution)/shard_map/ppermute | solution.py:13
  24.9 13.1 %collective-permute-start.8 = (bf16[2,6,64,256]{3,2,1,0:T(8,128)(2,1)S(1)}, bf16[2,6,64,256]{3,2,1,0:T(8,128)(2,1)S(1)}, u32[]{:S(2)}, u32[]{:S(2)}) collective-permute-start(bf16[2,6,64,256]{3,2,1,0:T(8,128)(2,1)S(1)} %slice.318), channel_id=1, source_target_pairs={{32,0},{64,32},{96,64},{33,1},{65,33},{97,65},{34,2},{66,34},{98,6... | collective-permute-start | bytes 1179656 | tf_op jit(solution)/shard_map/ppermute | solution.py:24
  34.4 10.5 %collective-permute-start.2 = (bf16[2,6,64,256]{3,2,1,0:T(8,128)(2,1)S(1)}, bf16[2,6,64,256]{3,2,1,0:T(8,128)(2,1)S(1)}, u32[]{:S(2)}, u32[]{:S(2)}) collective-permute-start(bf16[2,6,64,256]{3,2,1,0:T(8,128)(2,1)S(1)} %slice.306), channel_id=1, source_target_pairs={{0,32},{32,64},{64,96},{1,33},{33,65},{65,97},{2,34},{34,66},{66,9... | collective-permute-start | bytes 1179656 | tf_op jit(solution)/shard_map/ppermute | solution.py:24
  46.9 2.5 copy-start.8
  47.0 2.5 copy-start.10
  48.4 2.4 copy-start.9
  57.8 101.2 %collective-permute-start.3 = (bf16[4,1,64,256]{3,2,1,0:T(8,128)(2,1)S(1)}, bf16[4,1,64,256]{3,2,1,0:T(8,128)(2,1)S(1)}, u32[]{:S(2)}, u32[]{:S(2)}) collective-permute-start(bf16[4,1,64,256]{3,2,1,0:T(8,128)(2,1)S(1)} %get-tuple-element.16), channel_id=1, source_target_pairs={{0,1},{1,2},{2,3},{3,4},{4,5},{5,6},{6,7},{7,8},{8,9},{9,10},{10,1... | collective-permute-start | bytes 393224 | tf_op jit(solution)/shard_map/ppermute | solution.py:13
  59.6 99.3 %collective-permute-start.4 = (bf16[4,1,64,256]{3,2,1,0:T(8,128)(2,1)S(1)}, bf16[4,1,64,256]{3,2,1,0:T(8,128)(2,1)S(1)}, u32[]{:S(2)}, u32[]{:S(2)}) collective-permute-start(bf16[4,1,64,256]{3,2,1,0:T(8,128)(2,1)S(1)} %get-tuple-element.17), channel_id=1, source_target_pairs={{1,0},{2,1},{3,2},{4,3},{5,4},{6,5},{7,6},{8,7},{9,8},{10,9},{11,1... | collective-permute-start | bytes 393224 | tf_op jit(solution)/shard_map/ppermute | solution.py:16
  61.0 104.6 %collective-permute-start.9 = (bf16[4,1,64,256]{3,2,1,0:T(8,128)(2,1)S(1)}, bf16[4,1,64,256]{3,2,1,0:T(8,128)(2,1)S(1)}, u32[]{:S(2)}, u32[]{:S(2)}) collective-permute-start(bf16[4,1,64,256]{3,2,1,0:T(8,128)(2,1)S(1)} %get-tuple-element.12), channel_id=1, source_target_pairs={{0,1},{1,2},{2,3},{3,4},{4,5},{5,6},{6,7},{7,8},{8,9},{9,10},{10,1... | collective-permute-start | bytes 393224 | tf_op jit(solution)/shard_map/ppermute | solution.py:13
  65.0 100.6 %collective-permute-start.10 = (bf16[4,1,64,256]{3,2,1,0:T(8,128)(2,1)S(1)}, bf16[4,1,64,256]{3,2,1,0:T(8,128)(2,1)S(1)}, u32[]{:S(2)}, u32[]{:S(2)}) collective-permute-start(bf16[4,1,64,256]{3,2,1,0:T(8,128)(2,1)S(1)} %get-tuple-element.13), channel_id=1, source_target_pairs={{1,0},{2,1},{3,2},{4,3},{5,4},{6,5},{7,6},{8,7},{9,8},{10,9},{11,1... | collective-permute-start | bytes 393224 | tf_op jit(solution)/shard_map/ppermute | solution.py:16
  159.0 9.4 %collective-permute-start.5 = (bf16[2,6,64,256]{3,2,1,0:T(8,128)(2,1)S(1)}, bf16[2,6,64,256]{3,2,1,0:T(8,128)(2,1)S(1)}, u32[]{:S(2)}, u32[]{:S(2)}) collective-permute-start(bf16[2,6,64,256]{3,2,1,0:T(8,128)(2,1)S(1)} %pad_maximum_fusion.7), channel_id=1, source_target_pairs={{0,32},{32,64},{64,96},{1,33},{33,65},{65,97},{2,34},{34,66},{66,9... | collective-permute-start | bytes 1179656 | tf_op jit(solution)/shard_map/ppermute | solution.py:24
  166.4 13.9 %collective-permute-start.11 = (bf16[2,6,64,256]{3,2,1,0:T(8,128)(2,1)}, bf16[2,6,64,256]{3,2,1,0:T(8,128)(2,1)S(1)}, u32[]{:S(2)}, u32[]{:S(2)}) collective-permute-start(bf16[2,6,64,256]{3,2,1,0:T(8,128)(2,1)} %pad_maximum_fusion.5), channel_id=1, source_target_pairs={{32,0},{64,32},{96,64},{33,1},{65,33},{97,65},{34,2},{66,34},{98,6... | collective-permute-start | bytes 1179656 | tf_op jit(solution)/shard_map/ppermute | solution.py:24
  168.9 1.9 copy-start.2
  170.9 3.0 copy-start
  182.6 2.9 copy-start.1
  186.5 8.4 %slice-start = ((s8[7077888]{0:T(1024)(128)(4,1)}), s8[2883584]{0:T(1024)(128)(4,1)S(1)}, s32[]{:S(2)}) async-start(s8[7077888]{0:T(1024)(128)(4,1)} %bitcast.187), calls=%async_computation.1 | async-start | bytes 5767168
  186.5 3.9 %copy-start.4 = (bf16[4,4,64,256]{3,2,1,0:T(8,128)(2,1)S(1)}, bf16[4,4,64,256]{3,2,1,0:T(8,128)(2,1)}, u32[]{:S(2)}) copy-start(bf16[4,4,64,256]{3,2,1,0:T(8,128)(2,1)} %param.5) | copy-start | bytes 1572868
  186.5 8.4 %copy-start.7 = (bf16[1,3,3,64,64]{4,3,2,1,0:T(8,128)(2,1)S(1)}, bf16[1,3,3,64,64]{4,3,2,1,0:T(8,128)(2,1)}, u32[]{:S(2)}) copy-start(bf16[1,3,3,64,64]{4,3,2,1,0:T(8,128)(2,1)} %get-tuple-element.25) | copy-start | bytes 221188
  186.6 8.4 %slice-start.1 = ((s8[7077888]{0:T(1024)(128)(4,1)}), s8[4194304]{0:T(1024)(128)(4,1)S(1)}, s32[]{:S(2)}) async-start(s8[7077888]{0:T(1024)(128)(4,1)} %bitcast.187), calls=%async_computation.2 | async-start | bytes 8388608
  190.4 5.6 %copy-start.6 = (bf16[1,3,3,64,64]{4,3,2,1,0:T(8,128)(2,1)S(1)}, bf16[1,3,3,64,64]{4,3,2,1,0:T(8,128)(2,1)}, u32[]{:S(2)}) copy-start(bf16[1,3,3,64,64]{4,3,2,1,0:T(8,128)(2,1)} %get-tuple-element.24) | copy-start | bytes 221188
  194.9 2.2 copy-start.5
Sparse Core Ops, SparseCore 0:
  186.7 147.6 all-reduce.6
where the time goes:
time: 346 us; the launch traced here: 345 us
  waiting for transfers between devices  138 us (40%)
  blocking collectives  92.7 us (27%)
  starting transfers between devices  34.2 us (10%)
  matrix products  33.7 us (10%)
  local copies, waits for them, and re-layouts  25 us (7%)
  between operations  14.8 us (4%)
  other arithmetic  6.87 us (2%)
    psum x1, waiting for transfers between devices, per_device(): lax.psum((term_first, term_second, term_bias), ('frames', 'rows'))  135 us
    psum x1, blocking collectives, per_device(): lax.psum((term_first, term_second, term_bias), ('frames', 'rows'))  92.7 us
    dot_general x6, matrix products, forward_conv(): jnp.einsum('ok,frkw->frow', flat_kernel, taps[t:t + frame_count], preferr...  16.1 us
    ppermute x4, starting transfers between devices, with_halo(): lax.ppermute(lax.slice_in_dim(block, block.shape[dim] - width, None, axis...  15 us
    unnamed x58, local copies, waits for them, and re-layouts  14.3 us
    ppermute x4, starting transfers between devices, passed_along(): return lax.ppermute(value, axis, pairs)  13.9 us
    dot_general x6, matrix products, kernel_grad(): jnp.einsum('frow,frkw->ok', upstream, taps[t:t + frame_count], preferred_...  10 us
    dot_general x6, matrix products, adjoint_conv(): jnp.einsum('ck,frkw->frcw', flat_kernel, taps[2 - t:2 - t + frame_count],...  7.64 us
  transfers between devices with their start and end apart: 13, of which 2 were waited for; matrix products, arithmetic and copies ran while one was open for 12% of the time, Pallas kernels for 0%

commit v1 on v0

--- a/solution.py
+++ b/solution.py
@@ -122,8 +122,14 @@
     term_second = kernel_grad(cotangent, active_ext)
     term_first = kernel_grad(grad_pre, input_ext)
     term_bias = jnp.sum(grad_pre.astype(jnp.float32), axis=(0, 1, 3))
-    total_first, total_second, total_bias = lax.psum(
-        (term_first, term_second, term_bias), ("frames", "rows")
+
+    def _pass_pairs_all(packet, mesh_ax, dev_axis):
+        for u in (mesh_ax, dev_axis):
+            packet = lax.psum(packet, u)
+        return packet
+
+    total_first, total_second, total_bias = _pass_pairs_all(
+        (term_first, term_second, term_bias), "rows", "frames"
     )
     cell_total = (
         frame_count * lax.axis_size("frames") * row_count * lax.axis_size("rows") * col_count

time: 346 us -> 637 us (1.84)
  waiting for transfers between devices: 138 us -> 415 us
  blocking collectives: 92.7 us -> 99.2 us
    psum x1 -> x2, waiting for transfers between devices: 135 us -> 410 us  [_pass_pairs_all(): packet = lax.psum(packet, u)]
    psum x1 -> x2, blocking collectives: 92.7 us -> 99.2 us  [_pass_pairs_all(): packet = lax.psum(packet, u)]
    unnamed x58 -> x68, local copies, waits for them, and re-layouts: 14.3 us -> 15.7 us
  transfers between devices with their start and end apart: 13 -> 14, of which waited for: 2 -> 4; matrix products, arithmetic and copies ran while one was open for 12% -> 7% of each run, Pallas kernels for 0% -> 0%
where the time goes in v1:
time: 637 us
  waiting for transfers between devices  415 us (65%)
  blocking collectives  99.2 us (16%)
  matrix products  38.7 us (6%)
  starting transfers between devices  35.3 us (6%)
  local copies, waits for them, and re-layouts  27.1 us (4%)
  between operations  14.9 us (2%)
  other arithmetic  6.78 us (1%)
    psum x2, waiting for transfers between devices, _pass_pairs_all(): packet = lax.psum(packet, u)  410 us
    psum x2, blocking collectives, _pass_pairs_all(): packet = lax.psum(packet, u)  99.2 us
    ppermute x4, starting transfers between devices, with_halo(): lax.ppermute(lax.slice_in_dim(block, block.shape[dim] - width, None, axis...  16.8 us
    unnamed x68, local copies, waits for them, and re-layouts  15.7 us
    dot_general x6, matrix products, kernel_grad(): jnp.einsum('frow,frkw->ok', upstream, taps[t:t + frame_count], preferred_...  13.1 us
    dot_general x6, matrix products, forward_conv(): jnp.einsum('ok,frkw->frow', flat_kernel, taps[t:t + frame_count], preferr...  13.1 us
    ppermute x4, starting transfers between devices, passed_along(): return lax.ppermute(value, axis, pairs)  13 us
  transfers between devices with their start and end apart: 14, of which 4 were waited for; matrix products, arithmetic and copies ran while one was open for 7% of the time, Pallas kernels for 0%

profile of v1, /device:TPU:1, one launch (start us, length us, event | category | flops | bytes accessed | tf_op | source)
XLA Modules:
  0.0 636.7 jit_solution(13421554620196834452)
XLA Ops:
  7.2 1.0 fusion.59
  8.3 3.9 collective-permute-start
  12.2 1.3 collective-permute-start.1
  13.5 1.7 fusion.57
  15.2 4.6 collective-permute-start.6
  19.8 1.3 collective-permute-start.7
  21.1 2.0 fusion.60
  23.2 1.1 constant_dynamic-update-slice_fusion.1
  24.3 4.9 collective-permute-start.2
  29.3 2.0 fusion.61
  31.4 0.8 copy.32
  32.3 0.8 copy.36
  33.1 0.8 copy.34
  34.1 0.9 constant_dynamic-update-slice_fusion.5
  35.1 1.9 collective-permute-start.8
  37.5 0.3 fusion.33
  38.3 0.3 fusion.35
  39.0 0.3 fusion.37
  39.3 1.0 fusion.62
  40.4 1.0 fusion.63
  41.5 2.7 collective-permute-done.8
  45.0 0.3 fusion.46
  45.7 0.3 fusion.48
  46.5 1.0 fusion.65
  47.5 1.0 fusion.66
  48.6 1.3 multiply_convert_fusion
  49.9 1.5 convert_reduce_fusion
  51.4 2.1 fusion.4
  53.5 2.1 fusion.2
  55.6 4.3 collective-permute-start.3
  59.9 1.3 collective-permute-start.4
  61.2 2.1 fusion
  63.3 2.3 collective-permute-done.4
  65.6 0.8 pad_maximum_fusion.7
  66.4 3.3 collective-permute-start.5
  69.8 1.3 collective-permute-start.10
  71.1 4.0 collective-permute-start.9
  75.1 81.1 %psum.46 = f32[64]{0:T(128)S(1)} all-reduce(f32[64]{0:T(128)S(1)} %get-tuple-element.36), channel_id=1, replica_groups=mesh['frames'=4,'rows'=32] {'rows'}, use_global_device_ids=true, to_apply=%region_5.6 | all-reduce | flops 64 | bytes 512 | tf_op jit(solution)/shard_map/psum | solution.py:128
  156.2 18.0 %psum.47 = f32[64]{0:T(128)S(1)} all-reduce(f32[64]{0:T(128)S(1)} %psum.46), channel_id=1, replica_groups=mesh['frames'=4,'rows'=32] {'frames'}, use_global_device_ids=true, to_apply=%region_6.7 | all-reduce | flops 64 | bytes 512 | tf_op jit(solution)/shard_map/psum | solution.py:128
  174.3 0.5 broadcast_multiply_fusion.2
  174.8 0.8 pad_maximum_fusion.5
  175.6 2.8 collective-permute-start.11
  178.9 0.3 fusion.39
  179.6 0.3 fusion.41
  180.4 0.3 fusion.43
  180.7 1.5 convolution_bitcast_fusion.2
  182.2 1.4 copy-done
  183.6 1.5 convolution_bitcast_fusion.1
  185.4 3.8 convolution_bitcast_fusion
  190.3 0.3 fusion.52
  191.8 2.9 copy-done.1
  194.7 1.3 pad_maximum_fusion.3
  196.4 3.5 fusion.67
  200.0 3.5 convolution_add_fusion.1
  203.5 2.1 fusion.64
  205.6 1.9 fusion.17
  207.6 342.1 %all-reduce.9.cloned.1.call-done = (f32[3,3,3,64,64]{3,4,2,1,0:T(8,128)}, f32[3,3,3,64,64]{3,4,2,1,0:T(8,128)}) async-done(((f32[3,3,3,64,64]{3,4,2,1,0:T(8,128)}, f32[3,3,3,64,64]{3,4,2,1,0:T(8,128)}), (f32[3,3,3,64,64]{3,4,2,1,0:T(8,128)}, f32[3,3,3,64,64]{3,4,2,1,0:T(8,128)})) %all-reduce.9.cloned.1.call-update) | async-done | bytes 884752 | tf_op jit(solution)/shard_map/psum | solution.py:128
  549.7 3.4 convolution_add_fusion.4
  553.1 4.3 fusion.19
  557.4 67.5 %all-reduce.11.cloned.1.call-done = (f32[3,3,3,64,64]{3,4,2,1,0:T(8,128)}, f32[3,3,3,64,64]{3,4,2,1,0:T(8,128)}) async-done(((f32[3,3,3,64,64]{3,4,2,1,0:T(8,128)}, f32[3,3,3,64,64]{3,4,2,1,0:T(8,128)}), (f32[3,3,3,64,64]{3,4,2,1,0:T(8,128)}, f32[3,3,3,64,64]{3,4,2,1,0:T(8,128)})) %all-reduce.11.cloned.1.call-update) | async-done | bytes 884752 | tf_op jit(solution)/shard_map/psum | solution.py:128
  624.9 1.2 broadcast_multiply_fusion.1
  626.2 1.2 copy.52
  627.4 1.2 broadcast_multiply_fusion
  628.6 1.2 copy.53
  (95 shorter events, 7.5 us)
Async XLA Ops:
  7.2 27.8 %copy-start.2 = (bf16[4,4,64,256]{3,2,1,0:T(8,128)(2,1)S(1)}, bf16[4,4,64,256]{3,2,1,0:T(8,128)(2,1)}, u32[]{:S(2)}) copy-start(bf16[4,4,64,256]{3,2,1,0:T(8,128)(2,1)} %param.9) | copy-start | bytes 1572868
  7.2 542.5 %all-reduce.9.cloned.1.call-start = ((), (), s32[]{:S(2)}) async-start(), calls=%async_computation | async-start | bytes 3538944 | tf_op jit(solution)/shard_map/psum | solution.py:128
  8.3 14.9 %collective-permute-start = (bf16[4,1,64,256]{3,2,1,0:T(8,128)(2,1)S(1)}, bf16[4,1,64,256]{3,2,1,0:T(8,128)(2,1)S(1)}, u32[]{:S(2)}, u32[]{:S(2)}) collective-permute-start(bf16[4,1,64,256]{3,2,1,0:T(8,128)(2,1)S(1)} %get-tuple-element.21), channel_id=1, source_target_pairs={{0,1},{1,2},{2,3},{3,4},{4,5},{5,6},{6,7},{7,8},{8,9},{9,10},{10,1... | collective-permute-start | bytes 393224 | tf_op jit(solution)/shard_map/ppermute | solution.py:13
  12.2 12.0 %collective-permute-start.1 = (bf16[4,1,64,256]{3,2,1,0:T(8,128)(2,1)S(1)}, bf16[4,1,64,256]{3,2,1,0:T(8,128)(2,1)S(1)}, u32[]{:S(2)}, u32[]{:S(2)}) collective-permute-start(bf16[4,1,64,256]{3,2,1,0:T(8,128)(2,1)S(1)} %get-tuple-element.20), channel_id=1, source_target_pairs={{1,0},{2,1},{3,2},{4,3},{5,4},{6,5},{7,6},{8,7},{9,8},{10,9},{11,1... | collective-permute-start | bytes 393224 | tf_op jit(solution)/shard_map/ppermute | solution.py:16
  15.2 18.9 %collective-permute-start.6 = (bf16[4,1,64,256]{3,2,1,0:T(8,128)(2,1)}, bf16[4,1,64,256]{3,2,1,0:T(8,128)(2,1)}, u32[]{:S(2)}, u32[]{:S(2)}) collective-permute-start(bf16[4,1,64,256]{3,2,1,0:T(8,128)(2,1)} %get-tuple-element.17), channel_id=1, source_target_pairs={{0,1},{1,2},{2,3},{3,4},{4,5},{5,6},{6,7},{7,8},{8,9},{9,10},{10,1... | collective-permute-start | bytes 393224 | tf_op jit(solution)/shard_map/ppermute | solution.py:13
  19.8 15.2 %collective-permute-start.7 = (bf16[4,1,64,256]{3,2,1,0:T(8,128)(2,1)}, bf16[4,1,64,256]{3,2,1,0:T(8,128)(2,1)S(1)}, u32[]{:S(2)}, u32[]{:S(2)}) collective-permute-start(bf16[4,1,64,256]{3,2,1,0:T(8,128)(2,1)} %get-tuple-element.16), channel_id=1, source_target_pairs={{1,0},{2,1},{3,2},{4,3},{5,4},{6,5},{7,6},{8,7},{9,8},{10,9},{11,1... | collective-permute-start | bytes 393224 | tf_op jit(solution)/shard_map/ppermute | solution.py:16
  24.3 12.7 %collective-permute-start.2 = (bf16[2,6,64,256]{3,2,1,0:T(8,128)(2,1)S(1)}, bf16[2,6,64,256]{3,2,1,0:T(8,128)(2,1)S(1)}, u32[]{:S(2)}, u32[]{:S(2)}) collective-permute-start(bf16[2,6,64,256]{3,2,1,0:T(8,128)(2,1)S(1)} %slice.306), channel_id=1, source_target_pairs={{0,32},{32,64},{64,96},{1,33},{33,65},{65,97},{2,34},{34,66},{66,9... | collective-permute-start | bytes 1179656 | tf_op jit(solution)/shard_map/ppermute | solution.py:24
  35.1 9.1 %collective-permute-start.8 = (bf16[2,6,64,256]{3,2,1,0:T(8,128)(2,1)S(1)}, bf16[2,6,64,256]{3,2,1,0:T(8,128)(2,1)S(1)}, u32[]{:S(2)}, u32[]{:S(2)}) collective-permute-start(bf16[2,6,64,256]{3,2,1,0:T(8,128)(2,1)S(1)} %slice.318), channel_id=1, source_target_pairs={{32,0},{64,32},{96,64},{33,1},{65,33},{97,65},{34,2},{66,34},{98,6... | collective-permute-start | bytes 1179656 | tf_op jit(solution)/shard_map/ppermute | solution.py:24
  38.3 2.1 copy-start.7
  46.1 2.5 copy-start.13
  47.5 2.4 copy-start.12
  55.6 7.7 %collective-permute-start.3 = (bf16[4,1,64,256]{3,2,1,0:T(8,128)(2,1)S(1)}, bf16[4,1,64,256]{3,2,1,0:T(8,128)(2,1)S(1)}, u32[]{:S(2)}, u32[]{:S(2)}) collective-permute-start(bf16[4,1,64,256]{3,2,1,0:T(8,128)(2,1)S(1)} %get-tuple-element.18), channel_id=1, source_target_pairs={{0,1},{1,2},{2,3},{3,4},{4,5},{5,6},{6,7},{7,8},{8,9},{9,10},{10,1... | collective-permute-start | bytes 393224 | tf_op jit(solution)/shard_map/ppermute | solution.py:13
  59.9 5.7 collective-permute-start.4
  66.4 112.0 %collective-permute-start.5 = (bf16[2,6,64,256]{3,2,1,0:T(8,128)(2,1)}, bf16[2,6,64,256]{3,2,1,0:T(8,128)(2,1)S(1)}, u32[]{:S(2)}, u32[]{:S(2)}) collective-permute-start(bf16[2,6,64,256]{3,2,1,0:T(8,128)(2,1)} %pad_maximum_fusion.7), channel_id=1, source_target_pairs={{0,32},{32,64},{64,96},{1,33},{33,65},{65,97},{2,34},{34,66},{66,9... | collective-permute-start | bytes 1179656 | tf_op jit(solution)/shard_map/ppermute | solution.py:24
  69.8 105.0 %collective-permute-start.10 = (bf16[4,1,64,256]{3,2,1,0:T(8,128)(2,1)S(1)}, bf16[4,1,64,256]{3,2,1,0:T(8,128)(2,1)S(1)}, u32[]{:S(2)}, u32[]{:S(2)}) collective-permute-start(bf16[4,1,64,256]{3,2,1,0:T(8,128)(2,1)S(1)} %get-tuple-element.15), channel_id=1, source_target_pairs={{1,0},{2,1},{3,2},{4,3},{5,4},{6,5},{7,6},{8,7},{9,8},{10,9},{11,1... | collective-permute-start | bytes 393224 | tf_op jit(solution)/shard_map/ppermute | solution.py:16
  71.1 103.7 %collective-permute-start.9 = (bf16[4,1,64,256]{3,2,1,0:T(8,128)(2,1)S(1)}, bf16[4,1,64,256]{3,2,1,0:T(8,128)(2,1)S(1)}, u32[]{:S(2)}, u32[]{:S(2)}) collective-permute-start(bf16[4,1,64,256]{3,2,1,0:T(8,128)(2,1)S(1)} %get-tuple-element.14), channel_id=1, source_target_pairs={{0,1},{1,2},{2,3},{3,4},{4,5},{5,6},{6,7},{7,8},{8,9},{9,10},{10,1... | collective-permute-start | bytes 393224 | tf_op jit(solution)/shard_map/ppermute | solution.py:13
  175.6 13.8 %collective-permute-start.11 = (bf16[2,6,64,256]{3,2,1,0:T(8,128)(2,1)}, bf16[2,6,64,256]{3,2,1,0:T(8,128)(2,1)S(1)}, u32[]{:S(2)}, u32[]{:S(2)}) collective-permute-start(bf16[2,6,64,256]{3,2,1,0:T(8,128)(2,1)} %pad_maximum_fusion.5), channel_id=1, source_target_pairs={{32,0},{64,32},{96,64},{33,1},{65,33},{97,65},{34,2},{66,34},{98,6... | collective-permute-start | bytes 1179656 | tf_op jit(solution)/shard_map/ppermute | solution.py:24
  180.7 2.9 copy-start
  189.9 4.9 copy-start.9
  189.9 4.8 copy-start.10
  189.9 4.8 copy-start.11
  191.8 2.9 copy-start.1
  196.1 7.4 %slice-start = ((s8[7077888]{0:T(1024)(128)(4,1)}), s8[2883584]{0:T(1024)(128)(4,1)S(1)}, s32[]{:S(2)}) async-start(s8[7077888]{0:T(1024)(128)(4,1)} %bitcast.187), calls=%async_computation.2 | async-start | bytes 5767168
  196.1 428.8 %all-reduce.11.cloned.1.call-start = ((), (), s32[]{:S(2)}) async-start(), calls=%async_computation.1 | async-start | bytes 3538944 | tf_op jit(solution)/shard_map/psum | solution.py:128
  196.4 7.2 %copy-start.6 = (bf16[64,3,3,64]{0,3,2,1:T(8,128)(2,1)S(1)}, bf16[64,3,3,64]{0,3,2,1:T(8,128)(2,1)}, u32[]{:S(2)}) copy-start(bf16[64,3,3,64]{0,3,2,1:T(8,128)(2,1)} %copy.36) | copy-start | bytes 221188
  196.4 7.2 %slice-start.1 = ((s8[7077888]{0:T(1024)(128)(4,1)}), s8[4194304]{0:T(1024)(128)(4,1)S(1)}, s32[]{:S(2)}) async-start(s8[7077888]{0:T(1024)(128)(4,1)} %bitcast.187), calls=%async_computation.3 | async-start | bytes 8388608
  199.9 5.7 slice-start.2
  199.9 5.7 copy-start.8
  199.9 5.7 slice-start.3
  205.6 344.1 %copy-start.3 = (f32[4,4,256,64]{2,3,1,0:T(8,128)S(1)}, f32[4,4,256,64]{2,3,1,0:T(8,128)}, u32[]{:S(2)}) copy-start(f32[4,4,256,64]{2,3,1,0:T(8,128)} %fusion.64) | copy-start | bytes 3145732
  205.6 344.1 %copy-start.5 = (bf16[64,3,3,64]{0,3,2,1:T(8,128)(2,1)S(1)}, bf16[64,3,3,64]{0,3,2,1:T(8,128)(2,1)}, u32[]{:S(2)}) copy-start(bf16[64,3,3,64]{0,3,2,1:T(8,128)(2,1)} %copy.34) | copy-start | bytes 221188
  205.6 347.5 %copy-start.4 = (bf16[4,4,64,256]{3,2,1,0:T(8,128)(2,1)S(1)}, bf16[4,4,64,256]{3,2,1,0:T(8,128)(2,1)}, u32[]{:S(2)}) copy-start(bf16[4,4,64,256]{3,2,1,0:T(8,128)(2,1)} %param.5) | copy-start | bytes 1572868
Sparse Core Ops, SparseCore 0:
  196.2 353.4 all-reduce.8
  552.2 72.6 all-reduce.10
